TPU v7x, 512 devices: a whole 4x8x8 slice. The times are simulated.
512 devices in a mesh: tm: 32 (over y, x), blk: 16 (over z, core).
Axes of the slice: x: 4, y: 8, z: 8, core: 2. Of those that a mesh axis runs over, the one named last changes fastest.
Arguments:
- panel_strip: bfloat16 [32, 8192, 2304], P('tm', 'blk'), may hold values from -6 to 6
- pivot_inverses: bfloat16 [32, 2, 256, 256], P('tm'), may hold values from -0.0234375 to 0.0234375
- coupling: float32 [32, 256, 256], P('tm'), may hold values from -0.375 to 0.375
- pivot_nodes: int32 [3, 256], replicated, may hold values from 0 to 8191, as said below
Outputs:
- trailing: bfloat16 [32, 8192, 1792], P('tm', 'blk')
- reduced: float32 [32, 256, 256], P('tm')
Inputs may be any that keep to these rules, and one draw needn't show every extreme that they name: `pivot_nodes`: entry j of every row is a node of the range [(j // 16) * 512, (j // 16 + 1) * 512); all 768 entries differ.
All inputs are finite; a program needn't handle non-finite values.
Results may differ from a plain program's by a relative error of at most 0.0068.
Values may be sent and summed in bfloat16 or wider, within the bound.
No kernel may reach another device: no remote copies, remote signals or barrier semaphores. Data moves between devices by JAX's collectives and lax.ppermute only.
A program may use at most 128 MiB of HBM per device.

v0:
```python
import jax
import jax.numpy as jnp
from jax import lax
from jax.sharding import PartitionSpec as P


def passed_along(x, axis, by):
    count = lax.axis_size(axis)
    return lax.ppermute(x, axis, [(i, i + by) for i in range(count - by)])


def matmul_high(left, right):
    return jnp.dot(left, right, precision=lax.Precision.HIGHEST, preferred_element_type=jnp.float32)


def rounded_dot(left, right):
    return jnp.dot(left, right, preferred_element_type=jnp.float32).astype(jnp.bfloat16)


def reduced_by(block, factor, rows):
    product = jnp.dot(factor, rows, preferred_element_type=jnp.float32)
    return (block.astype(jnp.float32) - product).astype(jnp.bfloat16)


def body(panel_strip, pivot_inverses, coupling, pivot_nodes):
    strip = panel_strip[0]
    first_inverse, second_inverse = (pivot_inverses[0, 0], pivot_inverses[0, 1])
    coupling_here = coupling[0]
    w = coupling_here.shape[0]
    rows_here = strip.shape[0]
    per_device = w // lax.axis_size("blk")
    my_index = lax.axis_index("blk")
    local_rows = (
        lax.dynamic_slice_in_dim(pivot_nodes, my_index * per_device, per_device, 1)
        - my_index * rows_here
    ).reshape(-1)
    picker = (
        local_rows[:, None] == lax.broadcasted_iota(jnp.int32, (3 * per_device, rows_here), 1)
    ).astype(jnp.bfloat16)
    picked = rounded_dot(picker, strip)
    rows_one, rows_two, rows_edge = (
        picked[i * per_device : (i + 1) * per_device] for i in range(3)
    )
    near = lax.all_gather(
        jnp.concatenate(
            [
                rows_one[:, w : 3 * w],
                rows_two[:, :w],
                rows_two[:, 2 * w : 3 * w],
                rows_edge[:, : 3 * w],
            ],
            1,
        ),
        "blk",
        axis=0,
        tiled=True,
    )
    far = lax.all_gather(
        jnp.concatenate([rows_one[:, 3 * w :], rows_two[:, 3 * w :]], 1), "blk", axis=0, tiled=True
    )
    one_next, one_edge = (near[:, :w], near[:, w : 2 * w])
    two_panel, two_edge = (near[:, 2 * w : 3 * w], near[:, 3 * w : 4 * w])
    edge = near[:, 4 * w :]
    factor_at_two = rounded_dot(two_panel, first_inverse)
    factor_at_edge = rounded_dot(edge[:, :w], first_inverse)
    second_edge = reduced_by(two_edge, factor_at_two, one_edge)
    edge_updated = reduced_by(edge[:, w:], factor_at_edge, near[:, : 2 * w])
    edge_factor_two = rounded_dot(edge_updated[:, :w], second_inverse)
    boundary = reduced_by(edge_updated[:, w:], edge_factor_two, second_edge)
    count = lax.axis_size("tm")
    span = coupling_here
    current = boundary.astype(jnp.float32)
    step = 1
    while step < count:
        incoming = passed_along(current.astype(jnp.bfloat16), "tm", step).astype(jnp.float32)
        current = matmul_high(matmul_high(span, incoming), span.T) + current
        if 2 * step < count:
            span = matmul_high(span, passed_along(span, "tm", step))
        step *= 2
    reduced = current
    factor_one = rounded_dot(strip[:, :w], first_inverse)
    next_panel = reduced_by(strip[:, w : 2 * w], factor_one, one_next)
    factor_two = rounded_dot(next_panel, second_inverse)
    far_one, far_two = jnp.split(far, 2, 1)
    second_far = reduced_by(far_two, factor_at_two, far_one)
    one_rows = jnp.concatenate([one_edge, far_one], 1)
    two_rows = jnp.concatenate([second_edge, second_far], 1)
    updated = reduced_by(strip[:, 2 * w :], factor_one, one_rows)
    trailing = reduced_by(updated, factor_two, two_rows)
    return (trailing[None], reduced[None])


def solution(mesh):
    placed = (P("tm", "blk", None), P("tm", None, None, None), P("tm", None, None), P())
    return jax.shard_map(
        body,
        mesh=mesh,
        in_specs=placed,
        out_specs=(P("tm", "blk", None), P("tm", None, None)),
        check_vma=False,
    )
```

profile of v0, /device:TPU:40, one launch (start us, length us, event | category | flops | bytes accessed | tf_op | source)
XLA Modules:
  0.0 128.9 jit_solution(8305294757422915728)
XLA Ops:
  7.2 0.0 all-gather.2.cloned.1.call-start
  7.2 0.8 dynamic-slice_subtract_fusion
  8.0 0.1 eq.10
  8.1 2.2 %convolution_convert_fusion = bf16[48,2304]{1,0:T(8,128)(2,1)S(1)} fusion(s32[48]{0:T(128)S(1)} %eq.10, bf16[1,512,2304]{2,1,0:T(8,128)(2,1)} %param.4), kind=kOutput, calls=%fused_computation.2 | convolution fusion | flops 113381376 | bytes 2580672 | tf_op jit(solution)/shard_map/dot_general | solution.py:17
  10.3 0.6 pad_maximum_fusion
  11.0 3.4 %collective-permute-start = (f32[256,256]{1,0:T(8,128)S(1)}, f32[256,256]{1,0:T(8,128)}, u32[]{:S(2)}, u32[]{:S(2)}) collective-permute-start(f32[256,256]{1,0:T(8,128)S(1)} %bitcast.64), channel_id=1, source_target_pairs={{0,16},{16,32},{32,48},{48,64},{64,80},{80,96},{96,112},{112,128},... | collective-permute-start | bytes 786440 | tf_op jit(solution)/shard_map/ppermute | solution.py:9
  14.5 26.1 %all_gather.6 = bf16[256,1792]{1,0:T(8,128)(2,1)S(1)} all-gather(bf16[16,1792]{1,0:T(8,128)(2,1)S(1)} %pad_maximum_fusion.1), channel_id=1, replica_groups=mesh['tm'=32,'blk'=16] {'blk'}, dimensions={0}, use_global_device_ids=true | all-gather | bytes 974848 | tf_op jit(solution)/shard_map/all_gather | solution.py:44
  40.6 1.9 %convolution_convert_fusion.5 = bf16[256,256]{1,0:T(8,128)(2,1)} fusion(bf16[256,1792]{1,0:T(8,128)(2,1)S(1)} %all_gather.6, bf16[1,2,256,256]{3,2,1,0:T(8,128)(2,1)} %param.5), kind=kOutput, calls=%fused_computation.24 | convolution fusion | flops 33619968 | bytes 393216 | tf_op jit(solution)/shard_map/dot_general | solution.py:17
  42.5 2.0 %fusion.3 = bf16[256,512]{1,0:T(8,128)(2,1)} fusion(bf16[256,1792]{1,0:T(8,128)(2,1)S(1)} %all_gather.6, bf16[1,2,256,256]{3,2,1,0:T(8,128)(2,1)} %param.5), kind=kOutput, calls=%fused_computation.11 | convolution fusion | flops 101122048 | bytes 1048576 | tf_op jit(solution)/shard_map/dot_general | solution.py:21
  44.4 1.7 %fusion.5 = bf16[256,256]{1,0:T(8,128)(2,1)} fusion(bf16[256,256]{1,0:T(8,128)(2,1)} %convolution_convert_fusion.5, bf16[256,1792]{1,0:T(8,128)(2,1)S(1)} %all_gather.6), kind=kOutput, calls=%fused_computation.20 | convolution fusion | flops 33751040 | bytes 524288 | tf_op jit(solution)/shard_map/dot_general | solution.py:21
  46.2 2.1 %fusion.6 = bf16[256,256]{1,0:T(8,128)(2,1)} fusion(bf16[256,256]{1,0:T(8,128)(2,1)} %fusion.5, bf16[256,512]{1,0:T(8,128)(2,1)} %fusion.3, bf16[1,2,256,256]{3,2,1,0:T(8,128)(2,1)} %param.5), kind=kOutput, calls=%fused_computation.21 | convolution fusion | flops 67371008 | bytes 655360 | tf_op jit(solution)/shard_map/dot_general | solution.py:21
  48.3 3.5 %collective-permute-start.4 = (bf16[256,256]{1,0:T(8,128)(2,1)}, bf16[256,256]{1,0:T(8,128)(2,1)}, u32[]{:S(2)}, u32[]{:S(2)}) collective-permute-start(bf16[256,256]{1,0:T(8,128)(2,1)} %fusion.6), channel_id=1, source_target_pairs={{0,16},{16,32},{32,48},{48,64},{64,80},{80,96},{96,112},{112,128},... | collective-permute-start | bytes 393224 | tf_op jit(solution)/shard_map/ppermute | solution.py:9
  51.8 1.8 %convolution_convert_fusion.2 = bf16[512,256]{1,0:T(8,128)(2,1)} fusion(bf16[512,2304]{1,0:T(8,128)(2,1)S(1)} %bitcast.61, bf16[1,2,256,256]{3,2,1,0:T(8,128)(2,1)} %param.5), kind=kOutput, calls=%fused_computation.9 | convolution fusion | flops 67239936 | bytes 655360 | tf_op jit(solution)/shard_map/dot_general | solution.py:17
  53.6 2.1 %convolution_convert_fusion.1 = bf16[512,256]{1,0:T(8,128)(2,1)} fusion(bf16[512,256]{1,0:T(8,128)(2,1)} %convolution_convert_fusion.2, bf16[512,2304]{1,0:T(8,128)(2,1)S(1)} %bitcast.62, bf16[256,1792]{1,0:T(8,128)(2,1)S(1)} %all_gather.6, bf16[1,2,256,256]{3,2,1,0:T(8,128)(2,1)} %param.5), kind=kOutput, calls=%fused_computation.8 | convolution fusion | flops 134742016 | bytes 1048576 | tf_op jit(solution)/shard_map/dot_general | solution.py:17
  55.7 2.7 %collective-permute-done.4 = bf16[256,256]{1,0:T(8,128)(2,1)} collective-permute-done((bf16[256,256]{1,0:T(8,128)(2,1)}, bf16[256,256]{1,0:T(8,128)(2,1)}, u32[]{:S(2)}, u32[]{:S(2)}) %collective-permute-start.4) | collective-permute-done | bytes 131104 | tf_op jit(solution)/shard_map/ppermute | solution.py:9
  58.3 1.2 fusion.42
  59.6 1.5 %fusion.51 = (bf16[256,256]{1,0:T(8,128)(2,1)S(1)}, f32[256,256]{1,0:T(8,128)S(1)}) fusion(bf16[256,256]{1,0:T(8,128)(2,1)} %fusion.6, f32[256,256]{1,0:T(8,128)S(1)} %fusion.42, f32[1,256,256]{2,1,0:T(8,128)S(1)} %copy-done.1), kind=kOutput, calls=%fused_computation.66 | convolution fusion | flops 201523200 | bytes 1048576 | tf_op jit(solution)/shard_map/dot_general | solution.py:13
  61.1 2.6 %collective-permute-start.5 = (bf16[256,256]{1,0:T(8,128)(2,1)S(1)}, bf16[256,256]{1,0:T(8,128)(2,1)S(1)}, u32[]{:S(2)}, u32[]{:S(2)}) collective-permute-start(bf16[256,256]{1,0:T(8,128)(2,1)S(1)} %get-tuple-element.6), channel_id=1, source_target_pairs={{0,32},{16,48},{32,64},{48,80},{64,96},{80,112},{96,128},{112,144}... | collective-permute-start | bytes 393224 | tf_op jit(solution)/shard_map/ppermute | solution.py:9
  63.7 1.3 %fusion.44 = f32[256,256]{1,0:T(8,128)S(1)} fusion(f32[256,256]{1,0:T(8,128)} %collective-permute-done, f32[1,256,256]{2,1,0:T(8,128)S(1)} %copy-done.1), kind=kOutput, calls=%fused_computation.59 | convolution fusion | flops 201326592 | bytes 786432 | tf_op jit(solution)/shard_map/dot_general | solution.py:13
  65.0 4.7 %collective-permute-start.1 = (f32[256,256]{1,0:T(8,128)S(1)}, f32[256,256]{1,0:T(8,128)S(1)}, u32[]{:S(2)}, u32[]{:S(2)}) collective-permute-start(f32[256,256]{1,0:T(8,128)S(1)} %fusion.44), channel_id=1, source_target_pairs={{0,32},{16,48},{32,64},{48,80},{64,96},{80,112},{96,128},{112,144}... | collective-permute-start | bytes 786440 | tf_op jit(solution)/shard_map/ppermute | solution.py:9
  69.7 0.6 collective-permute-done.5
  70.4 0.3 fusion.58
  70.6 0.4 fusion.52
  71.0 2.4 %collective-permute-start.6 = (bf16[256,256]{1,0:T(8,128)(2,1)S(1)}, bf16[256,256]{1,0:T(8,128)(2,1)S(1)}, u32[]{:S(2)}, u32[]{:S(2)}) collective-permute-start(bf16[256,256]{1,0:T(8,128)(2,1)S(1)} %get-tuple-element.8), channel_id=1, source_target_pairs={{0,64},{16,80},{32,96},{48,112},{64,128},{80,144},{96,160},{112,17... | collective-permute-start | bytes 393224 | tf_op jit(solution)/shard_map/ppermute | solution.py:9
  73.5 4.7 %collective-permute-done.1 = f32[256,256]{1,0:T(8,128)S(1)} collective-permute-done((f32[256,256]{1,0:T(8,128)S(1)}, f32[256,256]{1,0:T(8,128)S(1)}, u32[]{:S(2)}, u32[]{:S(2)}) %collective-permute-start.1) | collective-permute-done | bytes 262176 | tf_op jit(solution)/shard_map/ppermute | solution.py:9
  78.2 0.4 fusion.55
  78.6 2.7 %collective-permute-start.2 = (f32[256,256]{1,0:T(8,128)S(1)}, f32[256,256]{1,0:T(8,128)S(1)}, u32[]{:S(2)}, u32[]{:S(2)}) collective-permute-start(f32[256,256]{1,0:T(8,128)S(1)} %fusion.55), channel_id=1, source_target_pairs={{0,64},{16,80},{32,96},{48,112},{64,128},{80,144},{96,160},{112,17... | collective-permute-start | bytes 786440 | tf_op jit(solution)/shard_map/ppermute | solution.py:9
  81.3 0.3 fusion.59
  81.5 0.4 fusion.53
  82.0 1.9 %collective-permute-start.7 = (bf16[256,256]{1,0:T(8,128)(2,1)S(1)}, bf16[256,256]{1,0:T(8,128)(2,1)S(1)}, u32[]{:S(2)}, u32[]{:S(2)}) collective-permute-start(bf16[256,256]{1,0:T(8,128)(2,1)S(1)} %get-tuple-element.10), channel_id=1, source_target_pairs={{0,128},{16,144},{32,160},{48,176},{64,192},{80,208},{96,224},{112... | collective-permute-start | bytes 393224 | tf_op jit(solution)/shard_map/ppermute | solution.py:9
  83.9 6.6 %collective-permute-done.2 = f32[256,256]{1,0:T(8,128)S(1)} collective-permute-done((f32[256,256]{1,0:T(8,128)S(1)}, f32[256,256]{1,0:T(8,128)S(1)}, u32[]{:S(2)}, u32[]{:S(2)}) %collective-permute-start.2) | collective-permute-done | bytes 262176 | tf_op jit(solution)/shard_map/ppermute | solution.py:9
  90.4 0.4 fusion.56
  90.8 1.9 %collective-permute-start.3 = (f32[256,256]{1,0:T(8,128)S(1)}, f32[256,256]{1,0:T(8,128)S(1)}, u32[]{:S(2)}, u32[]{:S(2)}) collective-permute-start(f32[256,256]{1,0:T(8,128)S(1)} %fusion.56), channel_id=1, source_target_pairs={{0,128},{16,144},{32,160},{48,176},{64,192},{80,208},{96,224},{112... | collective-permute-start | bytes 786440 | tf_op jit(solution)/shard_map/ppermute | solution.py:9
  92.8 11.0 %collective-permute-done.7 = bf16[256,256]{1,0:T(8,128)(2,1)S(1)} collective-permute-done((bf16[256,256]{1,0:T(8,128)(2,1)S(1)}, bf16[256,256]{1,0:T(8,128)(2,1)S(1)}, u32[]{:S(2)}, u32[]{:S(2)}) %collective-permute-start.7) | collective-permute-done | bytes 131104 | tf_op jit(solution)/shard_map/ppermute | solution.py:9
  103.7 0.3 fusion.60
  104.0 0.4 fusion.54
  104.4 1.3 %collective-permute-start.8 = (bf16[256,256]{1,0:T(8,128)(2,1)S(1)}, bf16[256,256]{1,0:T(8,128)(2,1)S(1)}, u32[]{:S(2)}, u32[]{:S(2)}) collective-permute-start(bf16[256,256]{1,0:T(8,128)(2,1)S(1)} %get-tuple-element.12), channel_id=1, source_target_pairs={{0,256},{16,272},{32,288},{48,304},{64,320},{80,336},{96,352},{112... | collective-permute-start | bytes 393224 | tf_op jit(solution)/shard_map/ppermute | solution.py:9
  105.7 1.3 collective-permute-done.3
  107.0 0.4 fusion.57
  107.4 7.8 %collective-permute-done.8 = bf16[256,256]{1,0:T(8,128)(2,1)S(1)} collective-permute-done((bf16[256,256]{1,0:T(8,128)(2,1)S(1)}, bf16[256,256]{1,0:T(8,128)(2,1)S(1)}, u32[]{:S(2)}, u32[]{:S(2)}) %collective-permute-start.8) | collective-permute-done | bytes 131104 | tf_op jit(solution)/shard_map/ppermute | solution.py:9
  115.2 0.3 fusion.61
  115.5 1.1 fusion.4
  116.6 1.2 split.8
  117.8 0.6 subtract_convert_fusion.1
  118.4 0.7 copy-done.3
  119.2 0.4 fusion.1
  119.6 0.6 copy-done.4
  120.2 1.9 %fusion = bf16[1,512,1792]{2,1,0:T(8,128)(2,1)} fusion(bf16[512,256]{1,0:T(8,128)(2,1)S(1)} %copy-done.4, bf16[512,1792]{1,0:T(8,128)(2,1)S(1)} %subtract_convert_fusion.1, bf16[256,1536]{1,0:T(8,128)(2,1)S(1)} %fusion.1, bf16[256,256]{1,0:T(8,128)(2,1)S(1)} %copy-done.7), kind=kOutput, calls=%fused_computation.4 | convolution fusion | flops 474349568 | bytes 4849664 | tf_op jit(solution)/shard_map/dot_general | solution.py:21
  (25 shorter events, 0.1 us)
Async XLA Ops:
  7.2 3.8 %copy-start.1 = (f32[1,256,256]{2,1,0:T(8,128)S(1)}, f32[1,256,256]{2,1,0:T(8,128)}, u32[]{:S(2)}) copy-start(f32[1,256,256]{2,1,0:T(8,128)} %param.6) | copy-start | bytes 786436
  7.2 109.4 %all-gather.2.cloned.1.call-start = ((), (), s32[]{:S(2)}) async-start(), calls=%async_computation | async-start | bytes 1671168 | tf_op jit(solution)/shard_map/all_gather | solution.py:58
  11.0 52.7 %collective-permute-start = (f32[256,256]{1,0:T(8,128)S(1)}, f32[256,256]{1,0:T(8,128)}, u32[]{:S(2)}, u32[]{:S(2)}) collective-permute-start(f32[256,256]{1,0:T(8,128)S(1)} %bitcast.64), channel_id=1, source_target_pairs={{0,16},{16,32},{32,48},{48,64},{64,80},{80,96},{96,112},{112,128},... | collective-permute-start | bytes 786440 | tf_op jit(solution)/shard_map/ppermute | solution.py:9
  14.5 37.3 %copy-start = (bf16[1,512,2304]{2,1,0:T(8,128)(2,1)S(1)}, bf16[1,512,2304]{2,1,0:T(8,128)(2,1)}, u32[]{:S(2)}) copy-start(bf16[1,512,2304]{2,1,0:T(8,128)(2,1)} %param.4) | copy-start | bytes 7077892
  40.6 15.1 %copy-start.2 = (bf16[256,1792]{1,0:T(8,128)(2,1)}, bf16[256,1792]{1,0:T(8,128)(2,1)S(1)}, u32[]{:S(2)}) copy-start(bf16[256,1792]{1,0:T(8,128)(2,1)S(1)} %all_gather.6) | copy-start | bytes 2752516
  48.3 10.1 %collective-permute-start.4 = (bf16[256,256]{1,0:T(8,128)(2,1)}, bf16[256,256]{1,0:T(8,128)(2,1)}, u32[]{:S(2)}, u32[]{:S(2)}) collective-permute-start(bf16[256,256]{1,0:T(8,128)(2,1)} %fusion.6), channel_id=1, source_target_pairs={{0,16},{16,32},{32,48},{48,64},{64,80},{80,96},{96,112},{112,128},... | collective-permute-start | bytes 393224 | tf_op jit(solution)/shard_map/ppermute | solution.py:9
  61.1 9.3 %collective-permute-start.5 = (bf16[256,256]{1,0:T(8,128)(2,1)S(1)}, bf16[256,256]{1,0:T(8,128)(2,1)S(1)}, u32[]{:S(2)}, u32[]{:S(2)}) collective-permute-start(bf16[256,256]{1,0:T(8,128)(2,1)S(1)} %get-tuple-element.6), channel_id=1, source_target_pairs={{0,32},{16,48},{32,64},{48,80},{64,96},{80,112},{96,128},{112,144}... | collective-permute-start | bytes 393224 | tf_op jit(solution)/shard_map/ppermute | solution.py:9
  65.0 13.2 %collective-permute-start.1 = (f32[256,256]{1,0:T(8,128)S(1)}, f32[256,256]{1,0:T(8,128)S(1)}, u32[]{:S(2)}, u32[]{:S(2)}) collective-permute-start(f32[256,256]{1,0:T(8,128)S(1)} %fusion.44), channel_id=1, source_target_pairs={{0,32},{16,48},{32,64},{48,80},{64,96},{80,112},{96,128},{112,144}... | collective-permute-start | bytes 786440 | tf_op jit(solution)/shard_map/ppermute | solution.py:9
  71.0 10.2 %collective-permute-start.6 = (bf16[256,256]{1,0:T(8,128)(2,1)S(1)}, bf16[256,256]{1,0:T(8,128)(2,1)S(1)}, u32[]{:S(2)}, u32[]{:S(2)}) collective-permute-start(bf16[256,256]{1,0:T(8,128)(2,1)S(1)} %get-tuple-element.8), channel_id=1, source_target_pairs={{0,64},{16,80},{32,96},{48,112},{64,128},{80,144},{96,160},{112,17... | collective-permute-start | bytes 393224 | tf_op jit(solution)/shard_map/ppermute | solution.py:9
  78.6 11.8 %collective-permute-start.2 = (f32[256,256]{1,0:T(8,128)S(1)}, f32[256,256]{1,0:T(8,128)S(1)}, u32[]{:S(2)}, u32[]{:S(2)}) collective-permute-start(f32[256,256]{1,0:T(8,128)S(1)} %fusion.55), channel_id=1, source_target_pairs={{0,64},{16,80},{32,96},{48,112},{64,128},{80,144},{96,160},{112,17... | collective-permute-start | bytes 786440 | tf_op jit(solution)/shard_map/ppermute | solution.py:9
  82.0 21.7 %collective-permute-start.7 = (bf16[256,256]{1,0:T(8,128)(2,1)S(1)}, bf16[256,256]{1,0:T(8,128)(2,1)S(1)}, u32[]{:S(2)}, u32[]{:S(2)}) collective-permute-start(bf16[256,256]{1,0:T(8,128)(2,1)S(1)} %get-tuple-element.10), channel_id=1, source_target_pairs={{0,128},{16,144},{32,160},{48,176},{64,192},{80,208},{96,224},{112... | collective-permute-start | bytes 393224 | tf_op jit(solution)/shard_map/ppermute | solution.py:9
  90.8 16.1 %collective-permute-start.3 = (f32[256,256]{1,0:T(8,128)S(1)}, f32[256,256]{1,0:T(8,128)S(1)}, u32[]{:S(2)}, u32[]{:S(2)}) collective-permute-start(f32[256,256]{1,0:T(8,128)S(1)} %fusion.56), channel_id=1, source_target_pairs={{0,128},{16,144},{32,160},{48,176},{64,192},{80,208},{96,224},{112... | collective-permute-start | bytes 786440 | tf_op jit(solution)/shard_map/ppermute | solution.py:9
  104.4 10.8 %collective-permute-start.8 = (bf16[256,256]{1,0:T(8,128)(2,1)S(1)}, bf16[256,256]{1,0:T(8,128)(2,1)S(1)}, u32[]{:S(2)}, u32[]{:S(2)}) collective-permute-start(bf16[256,256]{1,0:T(8,128)(2,1)S(1)} %get-tuple-element.12), channel_id=1, source_target_pairs={{0,256},{16,272},{32,288},{48,304},{64,320},{80,336},{96,352},{112... | collective-permute-start | bytes 393224 | tf_op jit(solution)/shard_map/ppermute | solution.py:9
  107.4 10.4 %slice-start = ((bf16[256,1792]{1,0:T(8,128)(2,1)}), bf16[256,256]{1,0:T(8,128)(2,1)S(1)}, s32[]{:S(2)}) async-start(bf16[256,1792]{1,0:T(8,128)(2,1)} %copy-done.2), calls=%async_computation.1 | async-start | bytes 262144 | tf_op jit(solution)/shard_map/slice | solution.py:61
  107.4 10.4 %copy-start.5 = (bf16[512,256]{1,0:T(8,128)(2,1)S(1)}, bf16[512,256]{1,0:T(8,128)(2,1)}, u32[]{:S(2)}) copy-start(bf16[512,256]{1,0:T(8,128)(2,1)} %convolution_convert_fusion.2) | copy-start | bytes 786436
  117.8 1.4 %copy-start.3 = (bf16[256,3072]{1,0:T(8,128)(2,1)S(1)}, bf16[256,3072]{1,0:T(8,128)(2,1)}, u32[]{:S(2)}) copy-start(bf16[256,3072]{1,0:T(8,128)(2,1)} %all-gather.2.cloned.1.call-done) | copy-start | bytes 4718596
  117.8 1.4 %copy-start.6 = (bf16[256,256]{1,0:T(8,128)(2,1)S(1)}, bf16[256,256]{1,0:T(8,128)(2,1)}, u32[]{:S(2)}) copy-start(bf16[256,256]{1,0:T(8,128)(2,1)} %convolution_convert_fusion.5) | copy-start | bytes 393220
  119.2 1.0 copy-start.4
  119.2 1.0 copy-start.7
Sparse Core Ops, SparseCore 0:
  11.1 46.6 all-gather.1
where the time goes:
time: 130 us; the launch traced here: 129 us
  waiting for transfers between devices  34.6 us (27%)
  blocking collectives  26.1 us (20%)
  matrix products  25.3 us (19%)
  starting transfers between devices  24.4 us (19%)
  between operations  14.4 us (11%)
  local copies, waits for them, and re-layouts  2.66 us (2%)
  other arithmetic  1.44 us (1%)
    ppermute x9, waiting for transfers between devices, passed_along(): return lax.ppermute(x, axis, [(i, i + by) for i in range(count - by)])  34.6 us
    all_gather x1, blocking collectives, body(): lax.all_gather(jnp.concatenate([rows_one[:, w:3 * w], rows_two[:, :w], ro...  26.1 us
    ppermute x9, starting transfers between devices, passed_along(): return lax.ppermute(x, axis, [(i, i + by) for i in range(count - by)])  24.4 us
    dot_general x6, matrix products, reduced_by(): product = jnp.dot(factor, rows, preferred_element_type=jnp.float32)  8.68 us
    dot_general x14, matrix products, matmul_high(): jnp.dot(left, right, precision=lax.Precision.HIGHEST, preferred_element_t...  8.61 us
    dot_general x4, matrix products, rounded_dot(): jnp.dot(left, right, preferred_element_type=jnp.float32)  7.99 us
  transfers between devices with their start and end apart: 10, of which 7 were waited for; matrix products, arithmetic and copies ran while one was open for 16% of the time, Pallas kernels for 0%

commit v1 on v0

--- a/solution.py
+++ b/solution.py
@@ -1,7 +1,16 @@
+import functools
 import jax
 import jax.numpy as jnp
 from jax import lax
 from jax.sharding import PartitionSpec as P
+
+
+def view_the_members_all(incoming_x, mesh_name):
+    p_next = jnp.stack(lax.axis_size(mesh_name) * [incoming_x])
+    return jnp.concatenate(lax.all_to_all(p_next, mesh_name, 0, 0), 0)
+
+
+clusters_reach = functools.partial(view_the_members_all, mesh_name="blk")
 
 
 def passed_along(x, axis, by):
@@ -41,7 +50,7 @@
     rows_one, rows_two, rows_edge = (
         picked[i * per_device : (i + 1) * per_device] for i in range(3)
     )
-    near = lax.all_gather(
+    near = clusters_reach(
         jnp.concatenate(
             [
                 rows_one[:, w : 3 * w],
@@ -50,10 +59,7 @@
                 rows_edge[:, : 3 * w],
             ],
             1,
-        ),
-        "blk",
-        axis=0,
-        tiled=True,
+        )
     )
     far = lax.all_gather(
         jnp.concatenate([rows_one[:, 3 * w :], rows_two[:, 3 * w :]], 1), "blk", axis=0, tiled=True

time: 130 us -> 137 us (1.054)
  the two profiles are of different devices: /device:TPU:40 before, /device:TPU:32 now
where the time goes in v1:
time: 137 us; the launch traced here: 136 us
  waiting for transfers between devices  55.1 us (40%)
  starting transfers between devices  33 us (24%)
  matrix products  28.1 us (21%)
  between operations  14.4 us (11%)
  local copies, waits for them, and re-layouts  4.37 us (3%)
  other arithmetic  1.4 us (1%)
    ppermute x9, waiting for transfers between devices, passed_along(): return lax.ppermute(x, axis, [(i, i + by) for i in range(count - by)])  37.8 us
    ppermute x9, starting transfers between devices, passed_along(): return lax.ppermute(x, axis, [(i, i + by) for i in range(count - by)])  22.4 us
    all_to_all x1, waiting for transfers between devices, view_the_members_all(): return jnp.concatenate(lax.all_to_all(p_next, mesh_name, 0, 0), 0)  17.3 us
    all_to_all x1, starting transfers between devices, view_the_members_all(): return jnp.concatenate(lax.all_to_all(p_next, mesh_name, 0, 0), 0)  10.6 us
    dot_general x14, matrix products, matmul_high(): jnp.dot(left, right, precision=lax.Precision.HIGHEST, preferred_element_t...  10.3 us
    dot_general x6, matrix products, reduced_by(): product = jnp.dot(factor, rows, preferred_element_type=jnp.float32)  9.82 us
    dot_general x4, matrix products, rounded_dot(): jnp.dot(left, right, preferred_element_type=jnp.float32)  7.92 us
  transfers between devices with their start and end apart: 11, of which 8 were waited for; matrix products, arithmetic and copies ran while one was open for 18% of the time, Pallas kernels for 0%

profile of v1, /device:TPU:32, one launch (start us, length us, event | category | flops | bytes accessed | tf_op | source)
XLA Modules:
  0.0 136.3 jit_solution(8794957937398210629)
XLA Ops:
  7.2 0.8 dynamic-slice_subtract_fusion
  8.0 2.2 %convolution_convert_fusion = bf16[48,2304]{1,0:T(8,128)(2,1)S(1)} fusion(s32[48]{0:T(128)S(1)} %eq.10, bf16[1,512,2304]{2,1,0:T(8,128)(2,1)} %param.4), kind=kOutput, calls=%fused_computation.2 | convolution fusion | flops 113381376 | bytes 2580672 | tf_op jit(solution)/shard_map/dot_general | solution.py:26
  10.3 1.0 stack.2
  11.3 10.6 %all-to-all-start = ((bf16[16,16,1792]{2,1,0:T(8,128)(2,1)}), bf16[16,16,1792]{2,1,0:T(8,128)(2,1)S(1)}, u32[]{:S(2)}, u32[]{:S(2)}) async-start(bf16[16,16,1792]{2,1,0:T(8,128)(2,1)} %stack.2), calls=%async_computation | async-start | bytes 1835008 | tf_op jit(solution)/shard_map/all_to_all | solution.py:10
  21.9 0.8 fusion.49
  22.8 0.6 pad_maximum_fusion
  23.4 3.4 %collective-permute-start = (f32[256,256]{1,0:T(8,128)S(1)}, f32[256,256]{1,0:T(8,128)}, u32[]{:S(2)}, u32[]{:S(2)}) collective-permute-start(f32[256,256]{1,0:T(8,128)S(1)} %bitcast.65), channel_id=1, source_target_pairs={{0,16},{16,32},{32,48},{48,64},{64,80},{80,96},{96,112},{112,128},... | collective-permute-start | bytes 786440 | tf_op jit(solution)/shard_map/ppermute | solution.py:18
  26.8 1.9 %convolution_convert_fusion.2 = bf16[512,256]{1,0:T(8,128)(2,1)} fusion(bf16[512,2304]{1,0:T(8,128)(2,1)S(1)} %bitcast.62, bf16[1,2,256,256]{3,2,1,0:T(8,128)(2,1)} %param.5), kind=kOutput, calls=%fused_computation.9 | convolution fusion | flops 67239936 | bytes 655360 | tf_op jit(solution)/shard_map/dot_general | solution.py:26
  28.7 17.3 %all-to-all-done = bf16[16,16,1792]{2,1,0:T(8,128)(2,1)S(1)} async-done(((bf16[16,16,1792]{2,1,0:T(8,128)(2,1)}), bf16[16,16,1792]{2,1,0:T(8,128)(2,1)S(1)}, u32[]{:S(2)}, u32[]{:S(2)}) %all-to-all-start) | async-done | bytes 917536 | tf_op jit(solution)/shard_map/all_to_all | solution.py:10
  46.0 1.7 %convolution_convert_fusion.5 = bf16[256,256]{1,0:T(8,128)(2,1)} fusion(bf16[256,1792]{1,0:T(8,128)(2,1)S(1)} %bitcast.66, bf16[1,2,256,256]{3,2,1,0:T(8,128)(2,1)} %param.5), kind=kOutput, calls=%fused_computation.24 | convolution fusion | flops 33619968 | bytes 393216 | tf_op jit(solution)/shard_map/dot_general | solution.py:26
  47.7 2.0 %fusion.3 = bf16[256,512]{1,0:T(8,128)(2,1)} fusion(bf16[256,1792]{1,0:T(8,128)(2,1)S(1)} %bitcast.67, bf16[1,2,256,256]{3,2,1,0:T(8,128)(2,1)} %param.5), kind=kOutput, calls=%fused_computation.11 | convolution fusion | flops 101122048 | bytes 1048576 | tf_op jit(solution)/shard_map/dot_general | solution.py:30
  49.7 1.8 %fusion.5 = bf16[256,256]{1,0:T(8,128)(2,1)} fusion(bf16[256,256]{1,0:T(8,128)(2,1)} %convolution_convert_fusion.5, bf16[256,1792]{1,0:T(8,128)(2,1)S(1)} %bitcast.68), kind=kOutput, calls=%fused_computation.20 | convolution fusion | flops 33751040 | bytes 524288 | tf_op jit(solution)/shard_map/dot_general | solution.py:30
  51.4 2.1 %fusion.6 = bf16[256,256]{1,0:T(8,128)(2,1)} fusion(bf16[256,256]{1,0:T(8,128)(2,1)} %fusion.5, bf16[256,512]{1,0:T(8,128)(2,1)} %fusion.3, bf16[1,2,256,256]{3,2,1,0:T(8,128)(2,1)} %param.5), kind=kOutput, calls=%fused_computation.21 | convolution fusion | flops 67371008 | bytes 655360 | tf_op jit(solution)/shard_map/dot_general | solution.py:30
  53.5 3.4 %collective-permute-start.4 = (bf16[256,256]{1,0:T(8,128)(2,1)}, bf16[256,256]{1,0:T(8,128)(2,1)S(1)}, u32[]{:S(2)}, u32[]{:S(2)}) collective-permute-start(bf16[256,256]{1,0:T(8,128)(2,1)} %fusion.6), channel_id=1, source_target_pairs={{0,16},{16,32},{32,48},{48,64},{64,80},{80,96},{96,112},{112,128},... | collective-permute-start | bytes 393224 | tf_op jit(solution)/shard_map/ppermute | solution.py:18
  57.0 1.3 fusion.44
  58.3 4.7 %collective-permute-start.1 = (f32[256,256]{1,0:T(8,128)S(1)}, f32[256,256]{1,0:T(8,128)S(1)}, u32[]{:S(2)}, u32[]{:S(2)}) collective-permute-start(f32[256,256]{1,0:T(8,128)S(1)} %fusion.44), channel_id=1, source_target_pairs={{0,32},{16,48},{32,64},{48,80},{64,96},{80,112},{96,128},{112,144}... | collective-permute-start | bytes 786440 | tf_op jit(solution)/shard_map/ppermute | solution.py:18
  63.0 2.0 %collective-permute-done.4 = bf16[256,256]{1,0:T(8,128)(2,1)S(1)} collective-permute-done((bf16[256,256]{1,0:T(8,128)(2,1)}, bf16[256,256]{1,0:T(8,128)(2,1)S(1)}, u32[]{:S(2)}, u32[]{:S(2)}) %collective-permute-start.4) | collective-permute-done | bytes 131104 | tf_op jit(solution)/shard_map/ppermute | solution.py:18
  65.0 0.3 fusion.42
  65.3 1.5 %fusion.51 = (bf16[256,256]{1,0:T(8,128)(2,1)S(1)}, f32[256,256]{1,0:T(8,128)S(1)}) fusion(bf16[256,256]{1,0:T(8,128)(2,1)} %fusion.6, f32[256,256]{1,0:T(8,128)S(1)} %fusion.42, f32[1,256,256]{2,1,0:T(8,128)S(1)} %copy-done.1), kind=kOutput, calls=%fused_computation.66 | convolution fusion | flops 201523200 | bytes 1048576 | tf_op jit(solution)/shard_map/dot_general | solution.py:22
  66.8 1.9 %collective-permute-start.5 = (bf16[256,256]{1,0:T(8,128)(2,1)S(1)}, bf16[256,256]{1,0:T(8,128)(2,1)S(1)}, u32[]{:S(2)}, u32[]{:S(2)}) collective-permute-start(bf16[256,256]{1,0:T(8,128)(2,1)S(1)} %get-tuple-element.6), channel_id=1, source_target_pairs={{0,32},{16,48},{32,64},{48,80},{64,96},{80,112},{96,128},{112,144}... | collective-permute-start | bytes 393224 | tf_op jit(solution)/shard_map/ppermute | solution.py:18
  68.8 4.2 %collective-permute-done.1 = f32[256,256]{1,0:T(8,128)S(1)} collective-permute-done((f32[256,256]{1,0:T(8,128)S(1)}, f32[256,256]{1,0:T(8,128)S(1)}, u32[]{:S(2)}, u32[]{:S(2)}) %collective-permute-start.1) | collective-permute-done | bytes 262176 | tf_op jit(solution)/shard_map/ppermute | solution.py:18
  73.0 0.4 fusion.55
  73.3 1.9 %collective-permute-start.2 = (f32[256,256]{1,0:T(8,128)S(1)}, f32[256,256]{1,0:T(8,128)S(1)}, u32[]{:S(2)}, u32[]{:S(2)}) collective-permute-start(f32[256,256]{1,0:T(8,128)S(1)} %fusion.55), channel_id=1, source_target_pairs={{0,64},{16,80},{32,96},{48,112},{64,128},{80,144},{96,160},{112,17... | collective-permute-start | bytes 786440 | tf_op jit(solution)/shard_map/ppermute | solution.py:18
  75.3 2.6 %collective-permute-done.5 = bf16[256,256]{1,0:T(8,128)(2,1)S(1)} collective-permute-done((bf16[256,256]{1,0:T(8,128)(2,1)S(1)}, bf16[256,256]{1,0:T(8,128)(2,1)S(1)}, u32[]{:S(2)}, u32[]{:S(2)}) %collective-permute-start.5) | collective-permute-done | bytes 131104 | tf_op jit(solution)/shard_map/ppermute | solution.py:18
  78.2 0.4 fusion.52
  78.6 1.9 %collective-permute-start.6 = (bf16[256,256]{1,0:T(8,128)(2,1)S(1)}, bf16[256,256]{1,0:T(8,128)(2,1)S(1)}, u32[]{:S(2)}, u32[]{:S(2)}) collective-permute-start(bf16[256,256]{1,0:T(8,128)(2,1)S(1)} %get-tuple-element.8), channel_id=1, source_target_pairs={{0,64},{16,80},{32,96},{48,112},{64,128},{80,144},{96,160},{112,17... | collective-permute-start | bytes 393224 | tf_op jit(solution)/shard_map/ppermute | solution.py:18
  80.5 5.1 %collective-permute-done.2 = f32[256,256]{1,0:T(8,128)S(1)} collective-permute-done((f32[256,256]{1,0:T(8,128)S(1)}, f32[256,256]{1,0:T(8,128)S(1)}, u32[]{:S(2)}, u32[]{:S(2)}) %collective-permute-start.2) | collective-permute-done | bytes 262176 | tf_op jit(solution)/shard_map/ppermute | solution.py:18
  85.6 0.4 fusion.56
  86.0 1.9 %collective-permute-start.3 = (f32[256,256]{1,0:T(8,128)S(1)}, f32[256,256]{1,0:T(8,128)S(1)}, u32[]{:S(2)}, u32[]{:S(2)}) collective-permute-start(f32[256,256]{1,0:T(8,128)S(1)} %fusion.56), channel_id=1, source_target_pairs={{0,128},{16,144},{32,160},{48,176},{64,192},{80,208},{96,224},{112... | collective-permute-start | bytes 786440 | tf_op jit(solution)/shard_map/ppermute | solution.py:18
  87.9 0.3 fusion.59
  88.2 0.4 fusion.53
  88.6 1.9 %collective-permute-start.7 = (bf16[256,256]{1,0:T(8,128)(2,1)S(1)}, bf16[256,256]{1,0:T(8,128)(2,1)S(1)}, u32[]{:S(2)}, u32[]{:S(2)}) collective-permute-start(bf16[256,256]{1,0:T(8,128)(2,1)S(1)} %get-tuple-element.10), channel_id=1, source_target_pairs={{0,128},{16,144},{32,160},{48,176},{64,192},{80,208},{96,224},{112... | collective-permute-start | bytes 393224 | tf_op jit(solution)/shard_map/ppermute | solution.py:18
  90.5 15.9 %collective-permute-done.3 = f32[256,256]{1,0:T(8,128)S(1)} collective-permute-done((f32[256,256]{1,0:T(8,128)S(1)}, f32[256,256]{1,0:T(8,128)S(1)}, u32[]{:S(2)}, u32[]{:S(2)}) %collective-permute-start.3) | collective-permute-done | bytes 262176 | tf_op jit(solution)/shard_map/ppermute | solution.py:18
  106.4 0.4 fusion.57
  106.8 0.7 slice.98
  107.5 0.4 collective-permute-done.7
  107.8 0.3 fusion.60
  108.1 1.2 fusion.54
  109.3 1.3 collective-permute-start.8
  110.6 2.1 %convolution_convert_fusion.1 = bf16[512,256]{1,0:T(8,128)(2,1)} fusion(bf16[512,256]{1,0:T(8,128)(2,1)} %convolution_convert_fusion.2, bf16[512,2304]{1,0:T(8,128)(2,1)S(1)} %bitcast.63, bf16[256,1792]{1,0:T(8,128)(2,1)S(1)} %bitcast.70, bf16[1,2,256,256]{3,2,1,0:T(8,128)(2,1)} %param.5), kind=kOutput, calls=%fused_computation.8 | convolution fusion | flops 134742016 | bytes 1048576 | tf_op jit(solution)/shard_map/dot_general | solution.py:26
  112.6 7.7 %collective-permute-done.8 = bf16[256,256]{1,0:T(8,128)(2,1)} collective-permute-done((bf16[256,256]{1,0:T(8,128)(2,1)}, bf16[256,256]{1,0:T(8,128)(2,1)}, u32[]{:S(2)}, u32[]{:S(2)}) %collective-permute-start.8) | collective-permute-done | bytes 131104 | tf_op jit(solution)/shard_map/ppermute | solution.py:18
  120.3 1.2 fusion.61
  121.5 2.1 %fusion.4 = f32[1,256,256]{2,1,0:T(8,128)} fusion(f32[256,256]{1,0:T(8,128)} %get-tuple-element.13, f32[256,256]{1,0:T(8,128)S(1)} %fusion.61, f32[256,256]{1,0:T(8,128)S(1)} %fusion.57), kind=kOutput, calls=%fused_computation.13 | convolution fusion | flops 201392128 | bytes 1048576 | tf_op jit(solution)/shard_map/dot_general | solution.py:22
  123.6 1.2 split.8
  124.8 1.7 %subtract_convert_fusion.1 = bf16[512,1792]{1,0:T(8,128)(2,1)S(1)} fusion(bf16[512,256]{1,0:T(8,128)(2,1)} %convolution_convert_fusion.2, bf16[512,2304]{1,0:T(8,128)(2,1)S(1)} %bitcast.64, bf16[256,1536]{1,0:T(8,128)(2,1)S(1)} %split.8, bf16[256,256]{1,0:T(8,128)(2,1)} %slice.98), kind=kOutput, calls=%fused_computation.1 | convolution fusion | flops 474349568 | bytes 4849664 | tf_op jit(solution)/shard_map/dot_general | solution.py:30
  126.6 0.4 fusion.1
  127.0 0.5 copy-done.4
  127.6 1.9 %fusion = bf16[1,512,1792]{2,1,0:T(8,128)(2,1)} fusion(bf16[512,256]{1,0:T(8,128)(2,1)S(1)} %copy-done.4, bf16[512,1792]{1,0:T(8,128)(2,1)S(1)} %subtract_convert_fusion.1, bf16[256,1536]{1,0:T(8,128)(2,1)S(1)} %fusion.1, bf16[256,256]{1,0:T(8,128)(2,1)S(1)} %copy-done.6), kind=kOutput, calls=%fused_computation.4 | convolution fusion | flops 474349568 | bytes 4849664 | tf_op jit(solution)/shard_map/dot_general | solution.py:30
  (24 shorter events, 0.5 us)
Async XLA Ops:
  10.2 1.1 copy-start.2
  10.3 13.2 %copy-start.1 = (f32[1,256,256]{2,1,0:T(8,128)S(1)}, f32[1,256,256]{2,1,0:T(8,128)}, u32[]{:S(2)}) copy-start(f32[1,256,256]{2,1,0:T(8,128)} %param.6) | copy-start | bytes 786436
  10.3 16.6 %copy-start = (bf16[1,512,2304]{2,1,0:T(8,128)(2,1)S(1)}, bf16[1,512,2304]{2,1,0:T(8,128)(2,1)}, u32[]{:S(2)}) copy-start(bf16[1,512,2304]{2,1,0:T(8,128)(2,1)} %param.4) | copy-start | bytes 7077892
  11.3 34.7 %all-to-all-start = ((bf16[16,16,1792]{2,1,0:T(8,128)(2,1)}), bf16[16,16,1792]{2,1,0:T(8,128)(2,1)S(1)}, u32[]{:S(2)}, u32[]{:S(2)}) async-start(bf16[16,16,1792]{2,1,0:T(8,128)(2,1)} %stack.2), calls=%async_computation | async-start | bytes 1835008 | tf_op jit(solution)/shard_map/all_to_all | solution.py:10
  21.9 101.7 %all-gather.2.cloned.1.call-start = ((), (), s32[]{:S(2)}) async-start(), calls=%async_computation.1 | async-start | bytes 1671168 | tf_op jit(solution)/shard_map/all_gather | solution.py:64
  23.4 33.5 %collective-permute-start = (f32[256,256]{1,0:T(8,128)S(1)}, f32[256,256]{1,0:T(8,128)}, u32[]{:S(2)}, u32[]{:S(2)}) collective-permute-start(f32[256,256]{1,0:T(8,128)S(1)} %bitcast.65), channel_id=1, source_target_pairs={{0,16},{16,32},{32,48},{48,64},{64,80},{80,96},{96,112},{112,128},... | collective-permute-start | bytes 786440 | tf_op jit(solution)/shard_map/ppermute | solution.py:18
  53.5 11.5 %collective-permute-start.4 = (bf16[256,256]{1,0:T(8,128)(2,1)}, bf16[256,256]{1,0:T(8,128)(2,1)S(1)}, u32[]{:S(2)}, u32[]{:S(2)}) collective-permute-start(bf16[256,256]{1,0:T(8,128)(2,1)} %fusion.6), channel_id=1, source_target_pairs={{0,16},{16,32},{32,48},{48,64},{64,80},{80,96},{96,112},{112,128},... | collective-permute-start | bytes 393224 | tf_op jit(solution)/shard_map/ppermute | solution.py:18
  58.3 14.7 %collective-permute-start.1 = (f32[256,256]{1,0:T(8,128)S(1)}, f32[256,256]{1,0:T(8,128)S(1)}, u32[]{:S(2)}, u32[]{:S(2)}) collective-permute-start(f32[256,256]{1,0:T(8,128)S(1)} %fusion.44), channel_id=1, source_target_pairs={{0,32},{16,48},{32,64},{48,80},{64,96},{80,112},{96,128},{112,144}... | collective-permute-start | bytes 786440 | tf_op jit(solution)/shard_map/ppermute | solution.py:18
  66.8 11.0 %collective-permute-start.5 = (bf16[256,256]{1,0:T(8,128)(2,1)S(1)}, bf16[256,256]{1,0:T(8,128)(2,1)S(1)}, u32[]{:S(2)}, u32[]{:S(2)}) collective-permute-start(bf16[256,256]{1,0:T(8,128)(2,1)S(1)} %get-tuple-element.6), channel_id=1, source_target_pairs={{0,32},{16,48},{32,64},{48,80},{64,96},{80,112},{96,128},{112,144}... | collective-permute-start | bytes 393224 | tf_op jit(solution)/shard_map/ppermute | solution.py:18
  73.3 12.3 %collective-permute-start.2 = (f32[256,256]{1,0:T(8,128)S(1)}, f32[256,256]{1,0:T(8,128)S(1)}, u32[]{:S(2)}, u32[]{:S(2)}) collective-permute-start(f32[256,256]{1,0:T(8,128)S(1)} %fusion.55), channel_id=1, source_target_pairs={{0,64},{16,80},{32,96},{48,112},{64,128},{80,144},{96,160},{112,17... | collective-permute-start | bytes 786440 | tf_op jit(solution)/shard_map/ppermute | solution.py:18
  78.6 9.3 %collective-permute-start.6 = (bf16[256,256]{1,0:T(8,128)(2,1)S(1)}, bf16[256,256]{1,0:T(8,128)(2,1)S(1)}, u32[]{:S(2)}, u32[]{:S(2)}) collective-permute-start(bf16[256,256]{1,0:T(8,128)(2,1)S(1)} %get-tuple-element.8), channel_id=1, source_target_pairs={{0,64},{16,80},{32,96},{48,112},{64,128},{80,144},{96,160},{112,17... | collective-permute-start | bytes 393224 | tf_op jit(solution)/shard_map/ppermute | solution.py:18
  86.0 20.4 %collective-permute-start.3 = (f32[256,256]{1,0:T(8,128)S(1)}, f32[256,256]{1,0:T(8,128)S(1)}, u32[]{:S(2)}, u32[]{:S(2)}) collective-permute-start(f32[256,256]{1,0:T(8,128)S(1)} %fusion.56), channel_id=1, source_target_pairs={{0,128},{16,144},{32,160},{48,176},{64,192},{80,208},{96,224},{112... | collective-permute-start | bytes 786440 | tf_op jit(solution)/shard_map/ppermute | solution.py:18
  88.6 19.2 %collective-permute-start.7 = (bf16[256,256]{1,0:T(8,128)(2,1)S(1)}, bf16[256,256]{1,0:T(8,128)(2,1)S(1)}, u32[]{:S(2)}, u32[]{:S(2)}) collective-permute-start(bf16[256,256]{1,0:T(8,128)(2,1)S(1)} %get-tuple-element.10), channel_id=1, source_target_pairs={{0,128},{16,144},{32,160},{48,176},{64,192},{80,208},{96,224},{112... | collective-permute-start | bytes 393224 | tf_op jit(solution)/shard_map/ppermute | solution.py:18
  109.3 11.1 %collective-permute-start.8 = (bf16[256,256]{1,0:T(8,128)(2,1)}, bf16[256,256]{1,0:T(8,128)(2,1)}, u32[]{:S(2)}, u32[]{:S(2)}) collective-permute-start(bf16[256,256]{1,0:T(8,128)(2,1)} %get-tuple-element.12), channel_id=1, source_target_pairs={{0,256},{16,272},{32,288},{48,304},{64,320},{80,336},{96,352},{112... | collective-permute-start | bytes 393224 | tf_op jit(solution)/shard_map/ppermute | solution.py:18
  124.8 1.8 %copy-start.3 = (bf16[256,3072]{1,0:T(8,128)(2,1)S(1)}, bf16[256,3072]{1,0:T(8,128)(2,1)}, u32[]{:S(2)}) copy-start(bf16[256,3072]{1,0:T(8,128)(2,1)} %all-gather.2.cloned.1.call-done) | copy-start | bytes 4718596
  124.8 1.8 %copy-start.5 = (bf16[256,256]{1,0:T(8,128)(2,1)S(1)}, bf16[256,256]{1,0:T(8,128)(2,1)}, u32[]{:S(2)}) copy-start(bf16[256,256]{1,0:T(8,128)(2,1)} %convolution_convert_fusion.5) | copy-start | bytes 393220
  126.6 1.0 copy-start.4
  126.6 1.0 copy-start.6
Sparse Core Ops, SparseCore 0:
  24.8 44.6 all-gather.1
